TPU v7x, 32 devices: a whole 2x2x4 slice. The times are simulated.
32 devices in a mesh: seq: 8 (over z, x), head: 2 (over y), dp: 2 (over core).
Axes of the slice: x: 2, y: 2, z: 4, core: 2. Of those that a mesh axis runs over, the one named last changes fastest.
Arguments:
- queries: bfloat16 [2, 2048, 1024], P('dp', 'seq', 'head'), may hold values from -6 to 6
- key_rows: bfloat16 [2, 2048, 1024], P('dp', 'seq', 'head'), may hold values from -6 to 6
- value_rows: bfloat16 [2, 2048, 1024], P('dp', 'seq', 'head'), may hold values from -140 to 140
- stretch_doc: int32 [2, 8], P('dp', 'seq'), may hold values from 0 to 3, never falling along the last dimension, each value on 1 to 4 neighbouring positions
- head_gain: float32 [8, 128], P('head'), may hold values from 0.1 to 1.9
- w_out: bfloat16 [1024, 2048], P('head'), may hold values from -0.1875 to 0.1875
- cotangent: bfloat16 [2, 2048, 2048], P('dp', 'seq'), may hold values from -40 to 40
Outputs:
- layer_out: bfloat16 [2, 2048, 2048], P('dp', ('seq', 'head'))
- query_grad: bfloat16 [2, 2048, 1024], P('dp', 'seq', 'head')
- key_grad: bfloat16 [2, 2048, 1024], P('dp', 'seq', 'head')
- value_grad: bfloat16 [2, 2048, 1024], P('dp', 'seq', 'head')
- gain_grad: float32 [8, 128], P('head')
Inputs may be any that keep to these rules, and one draw needn't show every extreme that they name: `stretch_doc`: document numbers never fall along a sequence; each document spans 1 to 4 whole stretches, and one spans exactly that many.
All inputs are finite; a program needn't handle non-finite values.
Results may differ from a plain program's by a relative error of at most 0.0055.
Values may be sent and summed in bfloat16 or wider, within the bound.
No kernel may reach another device: no remote copies, remote signals or barrier semaphores. Data moves between devices by JAX's collectives and lax.ppermute only.
A program may use at most 64 MiB of HBM per device.

v0:
```python
import math
import jax
import jax.numpy as jnp
from jax import lax
from jax.sharding import PartitionSpec as P

epsilon = 1e-05
highest = lax.Precision.HIGHEST


def shifted(block, axis, distance):
    devices = range(lax.axis_size(axis))
    route = [(i - distance, i) for i in devices if i - distance in devices]
    return lax.ppermute(block, axis, route)


def link_docs(earlier, following):
    sum_early, doc_early = earlier
    sum_late, doc_late = following
    merged = jnp.where(doc_early[0] == doc_late[0], sum_late + sum_early, sum_late)
    running = jnp.where(doc_late[0] < 0.5, sum_early, merged)
    return (running, jnp.where(doc_late < 0.5, doc_early, doc_late))


def double_chain(start, mover, seq_size):
    current = mover(start, 1)
    reach = 1
    while reach < seq_size - 1:
        current = link_docs(mover(current, reach), current)
        reach = reach * 2
    return current


def on_device(queries, key_rows, value_rows, stretch_doc, head_gain, w_out, cotangent):
    token_count = queries.shape[1]
    local_width = queries.shape[2]
    head_count = head_gain.shape[0]
    head_dim = head_gain.shape[1]
    stretches = stretch_doc.shape[1]
    stretch_len = token_count // stretches
    seq_size = lax.axis_size("seq")
    blocks = (stretches, stretch_len, head_count, head_dim)
    query_blk = queries[0].reshape(blocks)
    key_blk = key_rows[0].reshape(blocks)
    value_blk = value_rows[0].reshape(blocks)
    doc_ids = stretch_doc[0]
    doc_float = doc_ids.astype(jnp.float32) + 1.0
    stretch_order = jnp.arange(stretches)
    same_doc = doc_ids[:, None] == doc_ids[None, :]
    before_mask = jnp.where(
        same_doc & (stretch_order[None, :] < stretch_order[:, None]), 1.0, 0.0
    ).astype(jnp.float32)
    after_mask = jnp.where(
        same_doc & (stretch_order[None, :] > stretch_order[:, None]), 1.0, 0.0
    ).astype(jnp.float32)
    positions = jnp.arange(stretch_len)
    causal = positions[:, None] >= positions[None, :]

    def move_forward(pair, distance):
        return shifted((pair[0], pair[1]), "seq", distance)

    def move_backward(pair, distance):
        return shifted((pair[0], pair[1]), "seq", -distance)

    kv_sum = jnp.einsum("cshd,cshe->chde", key_blk, value_blk, preferred_element_type=jnp.float32)
    last_pick = jnp.where(doc_float == doc_float[0], 1.0, 0.0).astype(jnp.float32)
    own_state = jnp.einsum("c,chde->hde", last_pick, kv_sum, precision=highest)
    incoming, incoming_doc = double_chain((own_state, doc_float), move_forward, seq_size)
    take_in = jnp.where(doc_float == incoming_doc[0], 1.0, 0.0).astype(jnp.float32)
    states = (
        jnp.einsum("cj,jhde->chde", before_mask, kv_sum, precision=highest)
        + take_in[:, None, None, None] * incoming
    )
    scores = jnp.einsum("cthd,cshd->chts", query_blk, key_blk, preferred_element_type=jnp.float32)
    attn_weights = jnp.where(causal, scores, 0.0).astype(jnp.bfloat16)
    within = jnp.einsum(
        "chts,cshe->cthe", attn_weights, value_blk, preferred_element_type=jnp.float32
    )
    query_f = query_blk.astype(jnp.float32)
    carried = jnp.einsum("cthd,chde->cthe", query_f, states, precision=highest)
    attended = within + carried
    inv_rms = lax.rsqrt(jnp.mean(attended * attended, axis=-1, keepdims=True) + epsilon)
    unit_rows = attended * inv_rms
    normed_rows = (unit_rows * head_gain).astype(jnp.bfloat16).reshape(token_count, local_width)
    exchanged = lax.all_to_all(normed_rows, "head", split_axis=0, concat_axis=1, tiled=True)
    summed = jnp.dot(
        exchanged,
        lax.all_gather(w_out, "head", axis=0, tiled=True),
        preferred_element_type=jnp.float32,
    )
    layer_out = summed.astype(jnp.bfloat16)[None]
    grad_normed = jnp.einsum(
        "tm,fm->tf", cotangent[0], w_out, preferred_element_type=jnp.float32
    ).reshape(blocks)
    gain_part = jnp.sum(grad_normed * unit_rows, axis=(0, 1))
    total_tokens = seq_size * lax.axis_size("dp") * token_count
    gain_grad = lax.psum(gain_part, ("seq", "dp")) / math.sqrt(total_tokens)
    scaled = grad_normed * head_gain
    grad_attended = inv_rms * (
        scaled - unit_rows * jnp.mean(scaled * unit_rows, axis=-1, keepdims=True)
    )
    grad_bf = grad_attended.astype(jnp.bfloat16)
    query_term = jnp.einsum(
        "cthd,cthe->chde", query_blk, grad_bf, preferred_element_type=jnp.float32
    )
    first_pick = jnp.where(doc_float == doc_float[0], 1.0, 0.0).astype(jnp.float32)
    own_grad = jnp.einsum("c,chde->hde", first_pick, query_term, precision=highest)
    incoming_grad, grad_doc = double_chain((own_grad, doc_float), move_backward, seq_size)
    take_back = jnp.where(doc_float == grad_doc[0], 1.0, 0.0).astype(jnp.float32)
    grad_states = (
        jnp.einsum("cj,jhde->chde", after_mask, query_term, precision=highest)
        + take_back[:, None, None, None] * incoming_grad
    )
    grad_scores = jnp.einsum(
        "cthe,cshe->chts", grad_bf, value_blk, preferred_element_type=jnp.float32
    )
    grad_weights = jnp.where(causal, grad_scores, 0.0).astype(jnp.bfloat16)
    grad_f = grad_bf.astype(jnp.float32)
    query_grad = jnp.einsum(
        "chts,cshd->cthd", grad_weights, key_blk, preferred_element_type=jnp.float32
    ) + jnp.einsum("cthe,chde->cthd", grad_f, states, precision=highest)
    key_grad = jnp.einsum(
        "chts,cthd->cshd", grad_weights, query_blk, preferred_element_type=jnp.float32
    ) + jnp.einsum("cshe,chde->cshd", value_blk.astype(jnp.float32), grad_states, precision=highest)
    value_grad = jnp.einsum(
        "chts,cthe->cshe", attn_weights, grad_bf, preferred_element_type=jnp.float32
    ) + jnp.einsum("cshd,chde->cshe", key_blk.astype(jnp.float32), grad_states, precision=highest)
    out_shape = (1, token_count, local_width)
    return (
        layer_out,
        query_grad.astype(jnp.bfloat16).reshape(out_shape),
        key_grad.astype(jnp.bfloat16).reshape(out_shape),
        value_grad.astype(jnp.bfloat16).reshape(out_shape),
        gain_grad,
    )


def solution(mesh):
    return jax.shard_map(
        on_device,
        mesh=mesh,
        in_specs=(
            P("dp", "seq", "head"),
            P("dp", "seq", "head"),
            P("dp", "seq", "head"),
            P("dp", "seq"),
            P("head", None),
            P("head", None),
            P("dp", "seq", None),
        ),
        out_specs=(
            P("dp", ("seq", "head"), None),
            P("dp", "seq", "head"),
            P("dp", "seq", "head"),
            P("dp", "seq", "head"),
            P("head", None),
        ),
        check_vma=False,
    )
```

profile of v0, /device:TPU:7, one launch (start us, length us, event | category | flops | bytes accessed | tf_op | source)
XLA Modules:
  0.0 170.7 jit_solution(11719621536188737796)
XLA Ops:
  8.0 1.0 reshape.195
  9.2 1.0 reshape.196
  10.5 3.2 %collective-permute-start.4 = (f32[4,128,128]{2,1,0:T(8,128)S(1)}, f32[4,128,128]{2,1,0:T(8,128)S(1)}, u32[]{:S(2)}, u32[]{:S(2)}) collective-permute-start(f32[4,128,128]{2,1,0:T(8,128)S(1)} %get-tuple-element.19), channel_id=1, source_target_pairs={{0,4},{4,8},{8,12},{12,16},{16,20},{20,24},{24,28},{1,5},{5,9},{9,... | collective-permute-start | bytes 786440 | tf_op jit(solution)/shard_map/ppermute | solution.py:14
  13.6 5.9 %collective-permute-done.4 = f32[4,128,128]{2,1,0:T(8,128)S(1)} collective-permute-done((f32[4,128,128]{2,1,0:T(8,128)S(1)}, f32[4,128,128]{2,1,0:T(8,128)S(1)}, u32[]{:S(2)}, u32[]{:S(2)}) %collective-permute-start.4) | collective-permute-done | bytes 262176 | tf_op jit(solution)/shard_map/ppermute | solution.py:14
  19.5 4.0 %collective-permute-start.5 = (f32[4,128,128]{2,1,0:T(8,128)S(1)}, f32[4,128,128]{2,1,0:T(8,128)S(1)}, u32[]{:S(2)}, u32[]{:S(2)}) collective-permute-start(f32[4,128,128]{2,1,0:T(8,128)S(1)} %collective-permute-done.4), channel_id=1, source_target_pairs={{0,4},{4,8},{8,12},{12,16},{16,20},{20,24},{24,28},{1,5},{5,9},{9,... | collective-permute-start | bytes 786440 | tf_op jit(solution)/shard_map/ppermute | solution.py:14
  23.6 4.1 %collective-permute-start = (f32[1]{0:T(128)}, f32[1]{0:T(128)}, u32[]{:S(2)}, u32[]{:S(2)}) collective-permute-start(f32[1]{0:T(128)} %bitcast.1), channel_id=1, source_target_pairs={{0,4},{4,8},{8,12},{12,16},{16,20},{20,24},{24,28},{1,5},{5,9},{9,... | collective-permute-start | bytes 20 | tf_op jit(solution)/shard_map/ppermute | solution.py:14
  28.2 4.4 %collective-permute-start.1 = (f32[1]{0:T(128)}, f32[1]{0:T(128)}, u32[]{:S(2)}, u32[]{:S(2)}) collective-permute-start(f32[1]{0:T(128)} %collective-permute-done), channel_id=1, source_target_pairs={{0,4},{4,8},{8,12},{12,16},{16,20},{20,24},{24,28},{1,5},{5,9},{9,... | collective-permute-start | bytes 20 | tf_op jit(solution)/shard_map/ppermute | solution.py:14
  34.8 3.2 %collective-permute-start.6 = (f32[4,128,128]{2,1,0:T(8,128)S(1)}, f32[4,128,128]{2,1,0:T(8,128)S(1)}, u32[]{:S(2)}, u32[]{:S(2)}) collective-permute-start(f32[4,128,128]{2,1,0:T(8,128)S(1)} %fusion.14), channel_id=1, source_target_pairs={{0,8},{4,12},{8,16},{12,20},{16,24},{20,28},{1,9},{5,13},{9,17},{1... | collective-permute-start | bytes 786440 | tf_op jit(solution)/shard_map/ppermute | solution.py:14
  38.1 2.7 %fusion.7 = f32[256,512]{0,1:T(8,128)S(1)} fusion(bf16[512,2048]{1,0:T(8,128)(2,1)} %param.12, bf16[1,256,2048]{2,1,0:T(8,128)(2,1)S(1)} %copy-done), kind=kOutput, calls=%fused_computation.17 | convolution fusion | flops 536870912 | bytes 3670016 | tf_op jit(solution)/shard_map/tm,fm->tf/dot_general | solution.py:92
  42.0 3.9 %collective-permute-start.2 = (f32[1]{0:T(128)}, f32[1]{0:T(128)}, u32[]{:S(2)}, u32[]{:S(2)}) collective-permute-start(f32[1]{0:T(128)} %select_n.117), channel_id=1, source_target_pairs={{0,8},{4,12},{8,16},{12,20},{16,24},{20,28},{1,9},{5,13},{9,17},{1... | collective-permute-start | bytes 20 | tf_op jit(solution)/shard_map/ppermute | solution.py:14
  46.6 4.2 %collective-permute-start.7 = (f32[4,128,128]{2,1,0:T(8,128)S(1)}, f32[4,128,128]{2,1,0:T(8,128)S(1)}, u32[]{:S(2)}, u32[]{:S(2)}) collective-permute-start(f32[4,128,128]{2,1,0:T(8,128)S(1)} %fusion.13), channel_id=1, source_target_pairs={{0,16},{4,20},{8,24},{12,28},{1,17},{5,21},{9,25},{13,29},{2,18},{... | collective-permute-start | bytes 786440 | tf_op jit(solution)/shard_map/ppermute | solution.py:14
  52.1 2.1 %collective-permute-start.3 = (f32[1]{0:T(128)}, f32[1]{0:T(128)}, u32[]{:S(2)}, u32[]{:S(2)}) collective-permute-start(f32[1]{0:T(128)} %select_n.118), channel_id=1, source_target_pairs={{0,16},{4,20},{8,24},{12,28},{1,17},{5,21},{9,25},{13,29},{2,18},{... | collective-permute-start | bytes 20 | tf_op jit(solution)/shard_map/ppermute | solution.py:14
  57.4 4.2 %collective-permute-start.12 = (f32[4,128,128]{1,2,0:T(8,128)S(1)}, f32[4,128,128]{1,2,0:T(8,128)S(1)}, u32[]{:S(2)}, u32[]{:S(2)}) collective-permute-start(f32[4,128,128]{1,2,0:T(8,128)S(1)} %multiply_bitcast_fusion), channel_id=1, source_target_pairs={{4,0},{8,4},{12,8},{16,12},{20,16},{24,20},{28,24},{5,1},{9,5},{13... | collective-permute-start | bytes 786440 | tf_op jit(solution)/shard_map/ppermute | solution.py:14
  61.5 3.3 %collective-permute-start.8 = (f32[1]{0:T(128)}, f32[1]{0:T(128)}, u32[]{:S(2)}, u32[]{:S(2)}) collective-permute-start(f32[1]{0:T(128)} %bitcast.1), channel_id=1, source_target_pairs={{4,0},{8,4},{12,8},{16,12},{20,16},{24,20},{28,24},{5,1},{9,5},{13... | collective-permute-start | bytes 20 | tf_op jit(solution)/shard_map/ppermute | solution.py:14
  64.9 7.3 %collective-permute-done.8 = f32[1]{0:T(128)} collective-permute-done((f32[1]{0:T(128)}, f32[1]{0:T(128)}, u32[]{:S(2)}, u32[]{:S(2)}) %collective-permute-start.8) | collective-permute-done | bytes 36 | tf_op jit(solution)/shard_map/ppermute | solution.py:14
  72.1 1.9 %collective-permute-start.9 = (f32[1]{0:T(128)}, f32[1]{0:T(128)}, u32[]{:S(2)}, u32[]{:S(2)}) collective-permute-start(f32[1]{0:T(128)} %collective-permute-done.8), channel_id=1, source_target_pairs={{4,0},{8,4},{12,8},{16,12},{20,16},{24,20},{28,24},{5,1},{9,5},{13... | collective-permute-start | bytes 20 | tf_op jit(solution)/shard_map/ppermute | solution.py:14
  74.6 2.8 %collective-permute-done.9 = f32[1]{0:T(128)} collective-permute-done((f32[1]{0:T(128)}, f32[1]{0:T(128)}, u32[]{:S(2)}, u32[]{:S(2)}) %collective-permute-start.9) | collective-permute-done | bytes 36 | tf_op jit(solution)/shard_map/ppermute | solution.py:14
  78.7 1.3 collective-permute-start.10
  81.2 2.3 %collective-permute-done.10 = f32[1]{0:T(128)} collective-permute-done((f32[1]{0:T(128)}, f32[1]{0:T(128)}, u32[]{:S(2)}, u32[]{:S(2)}) %collective-permute-start.10) | collective-permute-done | bytes 36 | tf_op jit(solution)/shard_map/ppermute | solution.py:14
  84.1 1.3 collective-permute-start.11
  86.1 3.4 %collective-permute-done.11 = f32[1]{0:T(128)} collective-permute-done((f32[1]{0:T(128)}, f32[1]{0:T(128)}, u32[]{:S(2)}, u32[]{:S(2)}) %collective-permute-start.11) | collective-permute-done | bytes 36 | tf_op jit(solution)/shard_map/ppermute | solution.py:14
  90.8 1.9 %collective-permute-start.13 = (f32[4,128,128]{1,2,0:T(8,128)S(1)}, f32[4,128,128]{1,2,0:T(8,128)S(1)}, u32[]{:S(2)}, u32[]{:S(2)}) collective-permute-start(f32[4,128,128]{1,2,0:T(8,128)S(1)} %collective-permute-done.12), channel_id=1, source_target_pairs={{4,0},{8,4},{12,8},{16,12},{20,16},{24,20},{28,24},{5,1},{9,5},{13... | collective-permute-start | bytes 786440 | tf_op jit(solution)/shard_map/ppermute | solution.py:14
  93.4 5.4 %collective-permute-done.13 = f32[4,128,128]{1,2,0:T(8,128)S(1)} collective-permute-done((f32[4,128,128]{1,2,0:T(8,128)S(1)}, f32[4,128,128]{1,2,0:T(8,128)S(1)}, u32[]{:S(2)}, u32[]{:S(2)}) %collective-permute-start.13) | collective-permute-done | bytes 262176 | tf_op jit(solution)/shard_map/ppermute | solution.py:14
  98.9 1.3 collective-permute-start.14
  101.4 1.0 all_to_all.14
  103.1 3.4 %all-to-all-start = ((bf16[2,128,512]{1,2,0:T(8,128)(2,1)}), bf16[2,128,512]{1,2,0:T(8,128)(2,1)S(1)}, u32[]{:S(2)}, u32[]{:S(2)}) async-start(bf16[2,128,512]{1,2,0:T(8,128)(2,1)} %copy.39), calls=%async_computation | async-start | bytes 524288 | tf_op jit(solution)/shard_map/all_to_all | solution.py:85
  106.6 33.1 %psum.7 = f32[4,128]{1,0:T(4,128)S(1)} all-reduce(f32[4,128]{1,0:T(4,128)S(1)} %get-tuple-element.15), channel_id=1, replica_groups=mesh['seq'=8,'head'=2,'dp'=2] {'seq','dp'}, use_global_device_ids=true, to_apply=%region_3.4 | all-reduce | flops 512 | bytes 4096 | tf_op jit(solution)/shard_map/psum | solution.py:97
  140.0 1.0 fusion.10
  140.9 1.3 collective-permute-start.15
  142.8 1.3 convolution_bitcast_fusion
  144.1 13.4 %collective-permute-done.15 = f32[4,128,128]{1,2,0:T(8,128)S(1)} collective-permute-done((f32[4,128,128]{1,2,0:T(8,128)S(1)}, f32[4,128,128]{1,2,0:T(8,128)S(1)}, u32[]{:S(2)}, u32[]{:S(2)}) %collective-permute-start.15) | collective-permute-done | bytes 262176 | tf_op jit(solution)/shard_map/ppermute | solution.py:14
  160.2 3.7 %fusion = bf16[1,128,2048]{2,1,0:T(8,128)(2,1)} fusion(bf16[128,1024]{0,1:T(8,128)(2,1)S(1)} %bitcast.79, bf16[1024,2048]{1,0:T(8,128)(2,1)} %all-gather.2.cloned.1.call-done), kind=kOutput, calls=%fused_computation.1 | convolution fusion | flops 537133056 | bytes 4980736 | tf_op jit(solution)/shard_map/dot_general | solution.py:86
  (50 shorter events, 9.8 us)
Async XLA Ops:
  7.2 30.9 %copy-start = (bf16[1,256,2048]{2,1,0:T(8,128)(2,1)S(1)}, bf16[1,256,2048]{2,1,0:T(8,128)(2,1)}, u32[]{:S(2)}) copy-start(bf16[1,256,2048]{2,1,0:T(8,128)(2,1)} %param.13) | copy-start | bytes 3145732
  7.2 20.5 %copy-start.2 = (bf16[1,256,512]{2,1,0:T(8,128)(2,1)S(1)}, bf16[1,256,512]{2,1,0:T(8,128)(2,1)}, u32[]{:S(2)}) copy-start(bf16[1,256,512]{2,1,0:T(8,128)(2,1)} %param.7) | copy-start | bytes 786436
  7.2 153.0 %all-gather.2.cloned.1.call-start = ((), (), s32[]{:S(2)}) async-start(), calls=%async_computation.1 | async-start | bytes 6291456 | tf_op jit(solution)/shard_map/all_gather | solution.py:88
  10.5 9.1 %collective-permute-start.4 = (f32[4,128,128]{2,1,0:T(8,128)S(1)}, f32[4,128,128]{2,1,0:T(8,128)S(1)}, u32[]{:S(2)}, u32[]{:S(2)}) collective-permute-start(f32[4,128,128]{2,1,0:T(8,128)S(1)} %get-tuple-element.19), channel_id=1, source_target_pairs={{0,4},{4,8},{8,12},{12,16},{16,20},{20,24},{24,28},{1,5},{5,9},{9,... | collective-permute-start | bytes 786440 | tf_op jit(solution)/shard_map/ppermute | solution.py:14
  19.5 15.3 %collective-permute-start.5 = (f32[4,128,128]{2,1,0:T(8,128)S(1)}, f32[4,128,128]{2,1,0:T(8,128)S(1)}, u32[]{:S(2)}, u32[]{:S(2)}) collective-permute-start(f32[4,128,128]{2,1,0:T(8,128)S(1)} %collective-permute-done.4), channel_id=1, source_target_pairs={{0,4},{4,8},{8,12},{12,16},{16,20},{20,24},{24,28},{1,5},{5,9},{9,... | collective-permute-start | bytes 786440 | tf_op jit(solution)/shard_map/ppermute | solution.py:14
  23.6 4.6 %collective-permute-start = (f32[1]{0:T(128)}, f32[1]{0:T(128)}, u32[]{:S(2)}, u32[]{:S(2)}) collective-permute-start(f32[1]{0:T(128)} %bitcast.1), channel_id=1, source_target_pairs={{0,4},{4,8},{8,12},{12,16},{16,20},{20,24},{24,28},{1,5},{5,9},{9,... | collective-permute-start | bytes 20 | tf_op jit(solution)/shard_map/ppermute | solution.py:14
  28.2 5.3 %collective-permute-start.1 = (f32[1]{0:T(128)}, f32[1]{0:T(128)}, u32[]{:S(2)}, u32[]{:S(2)}) collective-permute-start(f32[1]{0:T(128)} %collective-permute-done), channel_id=1, source_target_pairs={{0,4},{4,8},{8,12},{12,16},{16,20},{20,24},{24,28},{1,5},{5,9},{9,... | collective-permute-start | bytes 20 | tf_op jit(solution)/shard_map/ppermute | solution.py:14
  34.8 21.2 %copy-start.3 = (f32[4,128]{1,0:T(4,128)S(1)}, f32[4,128]{1,0:T(4,128)}, u32[]{:S(2)}) copy-start(f32[4,128]{1,0:T(4,128)} %param.11) | copy-start | bytes 6148
  34.8 11.7 %collective-permute-start.6 = (f32[4,128,128]{2,1,0:T(8,128)S(1)}, f32[4,128,128]{2,1,0:T(8,128)S(1)}, u32[]{:S(2)}, u32[]{:S(2)}) collective-permute-start(f32[4,128,128]{2,1,0:T(8,128)S(1)} %fusion.14), channel_id=1, source_target_pairs={{0,8},{4,12},{8,16},{12,20},{16,24},{20,28},{1,9},{5,13},{9,17},{1... | collective-permute-start | bytes 786440 | tf_op jit(solution)/shard_map/ppermute | solution.py:14
  42.0 3.9 %collective-permute-start.2 = (f32[1]{0:T(128)}, f32[1]{0:T(128)}, u32[]{:S(2)}, u32[]{:S(2)}) collective-permute-start(f32[1]{0:T(128)} %select_n.117), channel_id=1, source_target_pairs={{0,8},{4,12},{8,16},{12,20},{16,24},{20,28},{1,9},{5,13},{9,17},{1... | collective-permute-start | bytes 20 | tf_op jit(solution)/shard_map/ppermute | solution.py:14
  46.6 8.8 %collective-permute-start.7 = (f32[4,128,128]{2,1,0:T(8,128)S(1)}, f32[4,128,128]{2,1,0:T(8,128)S(1)}, u32[]{:S(2)}, u32[]{:S(2)}) collective-permute-start(f32[4,128,128]{2,1,0:T(8,128)S(1)} %fusion.13), channel_id=1, source_target_pairs={{0,16},{4,20},{8,24},{12,28},{1,17},{5,21},{9,25},{13,29},{2,18},{... | collective-permute-start | bytes 786440 | tf_op jit(solution)/shard_map/ppermute | solution.py:14
  52.1 2.1 %collective-permute-start.3 = (f32[1]{0:T(128)}, f32[1]{0:T(128)}, u32[]{:S(2)}, u32[]{:S(2)}) collective-permute-start(f32[1]{0:T(128)} %select_n.118), channel_id=1, source_target_pairs={{0,16},{4,20},{8,24},{12,28},{1,17},{5,21},{9,25},{13,29},{2,18},{... | collective-permute-start | bytes 20 | tf_op jit(solution)/shard_map/ppermute | solution.py:14
  57.4 33.4 %collective-permute-start.12 = (f32[4,128,128]{1,2,0:T(8,128)S(1)}, f32[4,128,128]{1,2,0:T(8,128)S(1)}, u32[]{:S(2)}, u32[]{:S(2)}) collective-permute-start(f32[4,128,128]{1,2,0:T(8,128)S(1)} %multiply_bitcast_fusion), channel_id=1, source_target_pairs={{4,0},{8,4},{12,8},{16,12},{20,16},{24,20},{28,24},{5,1},{9,5},{13... | collective-permute-start | bytes 786440 | tf_op jit(solution)/shard_map/ppermute | solution.py:14
  61.5 10.6 %collective-permute-start.8 = (f32[1]{0:T(128)}, f32[1]{0:T(128)}, u32[]{:S(2)}, u32[]{:S(2)}) collective-permute-start(f32[1]{0:T(128)} %bitcast.1), channel_id=1, source_target_pairs={{4,0},{8,4},{12,8},{16,12},{20,16},{24,20},{28,24},{5,1},{9,5},{13... | collective-permute-start | bytes 20 | tf_op jit(solution)/shard_map/ppermute | solution.py:14
  72.1 5.3 %collective-permute-start.9 = (f32[1]{0:T(128)}, f32[1]{0:T(128)}, u32[]{:S(2)}, u32[]{:S(2)}) collective-permute-start(f32[1]{0:T(128)} %collective-permute-done.8), channel_id=1, source_target_pairs={{4,0},{8,4},{12,8},{16,12},{20,16},{24,20},{28,24},{5,1},{9,5},{13... | collective-permute-start | bytes 20 | tf_op jit(solution)/shard_map/ppermute | solution.py:14
  78.7 4.8 %collective-permute-start.10 = (f32[1]{0:T(128)}, f32[1]{0:T(128)}, u32[]{:S(2)}, u32[]{:S(2)}) collective-permute-start(f32[1]{0:T(128)} %select_n.135), channel_id=1, source_target_pairs={{8,0},{12,4},{16,8},{20,12},{24,16},{28,20},{9,1},{13,5},{17,9},{2... | collective-permute-start | bytes 20 | tf_op jit(solution)/shard_map/ppermute | solution.py:14
  84.1 5.4 %collective-permute-start.11 = (f32[1]{0:T(128)}, f32[1]{0:T(128)}, u32[]{:S(2)}, u32[]{:S(2)}) collective-permute-start(f32[1]{0:T(128)} %select_n.136), channel_id=1, source_target_pairs={{16,0},{20,4},{24,8},{28,12},{17,1},{21,5},{25,9},{29,13},{18,2},{... | collective-permute-start | bytes 20 | tf_op jit(solution)/shard_map/ppermute | solution.py:14
  90.8 8.0 %collective-permute-start.13 = (f32[4,128,128]{1,2,0:T(8,128)S(1)}, f32[4,128,128]{1,2,0:T(8,128)S(1)}, u32[]{:S(2)}, u32[]{:S(2)}) collective-permute-start(f32[4,128,128]{1,2,0:T(8,128)S(1)} %collective-permute-done.12), channel_id=1, source_target_pairs={{4,0},{8,4},{12,8},{16,12},{20,16},{24,20},{28,24},{5,1},{9,5},{13... | collective-permute-start | bytes 786440 | tf_op jit(solution)/shard_map/ppermute | solution.py:14
  93.1 7.4 %copy-start.1 = (bf16[4,256,256]{2,1,0:T(8,128)(2,1)}, bf16[4,256,256]{2,1,0:T(8,128)(2,1)S(1)}, u32[]{:S(2)}) copy-start(bf16[4,256,256]{2,1,0:T(8,128)(2,1)S(1)} %fusion.2) | copy-start | bytes 1572868
  98.9 41.1 %collective-permute-start.14 = (f32[4,128,128]{1,2,0:T(8,128)S(1)}, f32[4,128,128]{1,2,0:T(8,128)}, u32[]{:S(2)}, u32[]{:S(2)}) collective-permute-start(f32[4,128,128]{1,2,0:T(8,128)S(1)} %fusion.11), channel_id=1, source_target_pairs={{8,0},{12,4},{16,8},{20,12},{24,16},{28,20},{9,1},{13,5},{17,9},{2... | collective-permute-start | bytes 786440 | tf_op jit(solution)/shard_map/ppermute | solution.py:14
  103.1 57.0 %all-to-all-start = ((bf16[2,128,512]{1,2,0:T(8,128)(2,1)}), bf16[2,128,512]{1,2,0:T(8,128)(2,1)S(1)}, u32[]{:S(2)}, u32[]{:S(2)}) async-start(bf16[2,128,512]{1,2,0:T(8,128)(2,1)} %copy.39), calls=%async_computation | async-start | bytes 524288 | tf_op jit(solution)/shard_map/all_to_all | solution.py:85
  140.9 16.6 %collective-permute-start.15 = (f32[4,128,128]{1,2,0:T(8,128)S(1)}, f32[4,128,128]{1,2,0:T(8,128)S(1)}, u32[]{:S(2)}, u32[]{:S(2)}) collective-permute-start(f32[4,128,128]{1,2,0:T(8,128)S(1)} %fusion.10), channel_id=1, source_target_pairs={{16,0},{20,4},{24,8},{28,12},{17,1},{21,5},{25,9},{29,13},{18,2},{... | collective-permute-start | bytes 786440 | tf_op jit(solution)/shard_map/ppermute | solution.py:14
Sparse Core Ops, SparseCore 0:
  27.8 57.8 all-gather.1
where the time goes:
time: 172 us; the launch traced here: 171 us
  starting transfers between devices  49.1 us (29%)
  waiting for transfers between devices  41.2 us (24%)
  blocking collectives  33.1 us (19%)
  between operations  26.5 us (15%)
  matrix products  11.2 us (7%)
  local copies, waits for them, and re-layouts  6.59 us (4%)
  other arithmetic  2.95 us (2%)
    ppermute x16, starting transfers between devices, shifted(): return lax.ppermute(block, axis, route)  45.6 us
    ppermute x16, waiting for transfers between devices, shifted(): return lax.ppermute(block, axis, route)  41.2 us
    psum x1, blocking collectives, on_device(): gain_grad = lax.psum(gain_part, ('seq', 'dp')) / math.sqrt(total_tokens)  33.1 us
    dot_general x1, matrix products, on_device(): jnp.dot(exchanged, lax.all_gather(w_out, 'head', axis=0, tiled=True), pre...  3.72 us
  transfers between devices with their start and end apart: 18, of which 9 were waited for; matrix products, arithmetic and copies ran while one was open for 8% of the time, Pallas kernels for 0%

commit v1 on v0

--- a/solution.py
+++ b/solution.py
@@ -82,7 +82,12 @@
     inv_rms = lax.rsqrt(jnp.mean(attended * attended, axis=-1, keepdims=True) + epsilon)
     unit_rows = attended * inv_rms
     normed_rows = (unit_rows * head_gain).astype(jnp.bfloat16).reshape(token_count, local_width)
-    exchanged = lax.all_to_all(normed_rows, "head", split_axis=0, concat_axis=1, tiled=True)
+    exchanged = jnp.concatenate(
+        lax.all_to_all(
+            jnp.stack(jnp.split(normed_rows, lax.axis_size("head"), axis=0)), "head", 0, 0
+        ),
+        axis=1,
+    )
     summed = jnp.dot(
         exchanged,
         lax.all_gather(w_out, "head", axis=0, tiled=True),

time: 172 us -> 170 us (0.988)
  waiting for transfers between devices: 41.2 us -> 31.2 us
  starting transfers between devices: 49.1 us -> 55 us
  blocking collectives: 33.1 us -> 36.9 us
    ppermute x16, waiting for transfers between devices: 41.2 us -> 31.1 us  [shifted(): return lax.ppermute(block, axis, route)]
    ppermute x16, starting transfers between devices: 45.6 us -> 51.4 us  [shifted(): return lax.ppermute(block, axis, route)]
    psum x1, blocking collectives: 33.1 us -> 36.9 us  [on_device(): gain_grad = lax.psum(gain_part, ('seq', 'dp')) / math.sqrt(total_tokens)]
    all_to_all x2 -> x0, local copies, waits for them, and re-layouts: 1.76 us -> none  [on_device(): lax.all_to_all(normed_rows, 'head', split_axis=0, concat_axis=1, tiled=True)]
  transfers between devices with their start and end apart: 18 -> 18, of which waited for: 9 -> 7; matrix products, arithmetic and copies ran while one was open for 8% -> 8% of each run, Pallas kernels for 0% -> 0%
where the time goes in v1:
time: 170 us; the launch traced here: 169 us
  starting transfers between devices  55 us (32%)
  blocking collectives  36.9 us (22%)
  waiting for transfers between devices  31.2 us (18%)
  between operations  26.8 us (16%)
  matrix products  11.2 us (7%)
  local copies, waits for them, and re-layouts  4.88 us (3%)
  other arithmetic  2.98 us (2%)
    ppermute x16, starting transfers between devices, shifted(): return lax.ppermute(block, axis, route)  51.4 us
    psum x1, blocking collectives, on_device(): gain_grad = lax.psum(gain_part, ('seq', 'dp')) / math.sqrt(total_tokens)  36.9 us
    ppermute x16, waiting for transfers between devices, shifted(): return lax.ppermute(block, axis, route)  31.1 us
    dot_general x1, matrix products, on_device(): jnp.dot(exchanged, lax.all_gather(w_out, 'head', axis=0, tiled=True), pre...  3.72 us
    all_to_all x1, starting transfers between devices, on_device(): lax.all_to_all(jnp.stack(jnp.split(normed_rows, lax.axis_size('head'), ax...  3.56 us
  transfers between devices with their start and end apart: 18, of which 7 were waited for; matrix products, arithmetic and copies ran while one was open for 8% of the time, Pallas kernels for 0%

profile of v1, /device:TPU:7, one launch (start us, length us, event | category | flops | bytes accessed | tf_op | source)
XLA Modules:
  0.0 168.9 jit_solution(3950437468865324996)
XLA Ops:
  8.0 1.0 reshape.201
  9.2 1.0 reshape.202
  10.5 3.2 %collective-permute-start.4 = (f32[4,128,128]{2,1,0:T(8,128)S(1)}, f32[4,128,128]{2,1,0:T(8,128)S(1)}, u32[]{:S(2)}, u32[]{:S(2)}) collective-permute-start(f32[4,128,128]{2,1,0:T(8,128)S(1)} %get-tuple-element.16), channel_id=1, source_target_pairs={{0,4},{4,8},{8,12},{12,16},{16,20},{20,24},{24,28},{1,5},{5,9},{9,... | collective-permute-start | bytes 786440 | tf_op jit(solution)/shard_map/ppermute | solution.py:14
  13.6 5.9 %collective-permute-done.4 = f32[4,128,128]{2,1,0:T(8,128)S(1)} collective-permute-done((f32[4,128,128]{2,1,0:T(8,128)S(1)}, f32[4,128,128]{2,1,0:T(8,128)S(1)}, u32[]{:S(2)}, u32[]{:S(2)}) %collective-permute-start.4) | collective-permute-done | bytes 262176 | tf_op jit(solution)/shard_map/ppermute | solution.py:14
  19.5 4.0 %collective-permute-start.5 = (f32[4,128,128]{2,1,0:T(8,128)S(1)}, f32[4,128,128]{2,1,0:T(8,128)S(1)}, u32[]{:S(2)}, u32[]{:S(2)}) collective-permute-start(f32[4,128,128]{2,1,0:T(8,128)S(1)} %collective-permute-done.4), channel_id=1, source_target_pairs={{0,4},{4,8},{8,12},{12,16},{16,20},{20,24},{24,28},{1,5},{5,9},{9,... | collective-permute-start | bytes 786440 | tf_op jit(solution)/shard_map/ppermute | solution.py:14
  23.6 4.1 %collective-permute-start = (f32[1]{0:T(128)}, f32[1]{0:T(128)}, u32[]{:S(2)}, u32[]{:S(2)}) collective-permute-start(f32[1]{0:T(128)} %bitcast.1), channel_id=1, source_target_pairs={{0,4},{4,8},{8,12},{12,16},{16,20},{20,24},{24,28},{1,5},{5,9},{9,... | collective-permute-start | bytes 20 | tf_op jit(solution)/shard_map/ppermute | solution.py:14
  27.6 2.6 %collective-permute-start.8 = (f32[1]{0:T(128)}, f32[1]{0:T(128)}, u32[]{:S(2)}, u32[]{:S(2)}) collective-permute-start(f32[1]{0:T(128)} %bitcast.1), channel_id=1, source_target_pairs={{4,0},{8,4},{12,8},{16,12},{20,16},{24,20},{28,24},{5,1},{9,5},{13... | collective-permute-start | bytes 20 | tf_op jit(solution)/shard_map/ppermute | solution.py:14
  30.4 4.3 %collective-permute-start.1 = (f32[1]{0:T(128)}, f32[1]{0:T(128)}, u32[]{:S(2)}, u32[]{:S(2)}) collective-permute-start(f32[1]{0:T(128)} %collective-permute-done), channel_id=1, source_target_pairs={{0,4},{4,8},{8,12},{12,16},{16,20},{20,24},{24,28},{1,5},{5,9},{9,... | collective-permute-start | bytes 20 | tf_op jit(solution)/shard_map/ppermute | solution.py:14
  36.8 3.2 %collective-permute-start.6 = (f32[4,128,128]{2,1,0:T(8,128)S(1)}, f32[4,128,128]{2,1,0:T(8,128)S(1)}, u32[]{:S(2)}, u32[]{:S(2)}) collective-permute-start(f32[4,128,128]{2,1,0:T(8,128)S(1)} %fusion.14), channel_id=1, source_target_pairs={{0,8},{4,12},{8,16},{12,20},{16,24},{20,28},{1,9},{5,13},{9,17},{1... | collective-permute-start | bytes 786440 | tf_op jit(solution)/shard_map/ppermute | solution.py:14
  40.0 2.6 %fusion.7 = f32[256,512]{0,1:T(8,128)S(1)} fusion(bf16[512,2048]{1,0:T(8,128)(2,1)} %param.12, bf16[1,256,2048]{2,1,0:T(8,128)(2,1)S(1)} %copy-done), kind=kOutput, calls=%fused_computation.17 | convolution fusion | flops 536870912 | bytes 3670016 | tf_op jit(solution)/shard_map/tm,fm->tf/dot_general | solution.py:97
  43.9 3.9 %collective-permute-start.2 = (f32[1]{0:T(128)}, f32[1]{0:T(128)}, u32[]{:S(2)}, u32[]{:S(2)}) collective-permute-start(f32[1]{0:T(128)} %select_n.117), channel_id=1, source_target_pairs={{0,8},{4,12},{8,16},{12,20},{16,24},{20,28},{1,9},{5,13},{9,17},{1... | collective-permute-start | bytes 20 | tf_op jit(solution)/shard_map/ppermute | solution.py:14
  48.4 3.9 %collective-permute-start.7 = (f32[4,128,128]{2,1,0:T(8,128)S(1)}, f32[4,128,128]{2,1,0:T(8,128)S(1)}, u32[]{:S(2)}, u32[]{:S(2)}) collective-permute-start(f32[4,128,128]{2,1,0:T(8,128)S(1)} %fusion.13), channel_id=1, source_target_pairs={{0,16},{4,20},{8,24},{12,28},{1,17},{5,21},{9,25},{13,29},{2,18},{... | collective-permute-start | bytes 786440 | tf_op jit(solution)/shard_map/ppermute | solution.py:14
  53.0 4.6 %collective-permute-start.9 = (f32[1]{0:T(128)}, f32[1]{0:T(128)}, u32[]{:S(2)}, u32[]{:S(2)}) collective-permute-start(f32[1]{0:T(128)} %collective-permute-done.8), channel_id=1, source_target_pairs={{4,0},{8,4},{12,8},{16,12},{20,16},{24,20},{28,24},{5,1},{9,5},{13... | collective-permute-start | bytes 20 | tf_op jit(solution)/shard_map/ppermute | solution.py:14
  59.8 1.3 collective-permute-start.10
  62.9 5.1 %collective-permute-start.3 = (f32[1]{0:T(128)}, f32[1]{0:T(128)}, u32[]{:S(2)}, u32[]{:S(2)}) collective-permute-start(f32[1]{0:T(128)} %select_n.118), channel_id=1, source_target_pairs={{0,16},{4,20},{8,24},{12,28},{1,17},{5,21},{9,25},{13,29},{2,18},{... | collective-permute-start | bytes 20 | tf_op jit(solution)/shard_map/ppermute | solution.py:14
  68.8 1.3 collective-permute-start.11
  71.4 2.6 %collective-permute-done.11 = f32[1]{0:T(128)} collective-permute-done((f32[1]{0:T(128)}, f32[1]{0:T(128)}, u32[]{:S(2)}, u32[]{:S(2)}) %collective-permute-start.11) | collective-permute-done | bytes 36 | tf_op jit(solution)/shard_map/ppermute | solution.py:14
  77.3 3.9 %collective-permute-start.12 = (f32[4,128,128]{1,2,0:T(8,128)S(1)}, f32[4,128,128]{1,2,0:T(8,128)S(1)}, u32[]{:S(2)}, u32[]{:S(2)}) collective-permute-start(f32[4,128,128]{1,2,0:T(8,128)S(1)} %multiply_bitcast_fusion), channel_id=1, source_target_pairs={{4,0},{8,4},{12,8},{16,12},{20,16},{24,20},{28,24},{5,1},{9,5},{13... | collective-permute-start | bytes 786440 | tf_op jit(solution)/shard_map/ppermute | solution.py:14
  81.9 3.4 %collective-permute-done.12 = f32[4,128,128]{1,2,0:T(8,128)S(1)} collective-permute-done((f32[4,128,128]{1,2,0:T(8,128)S(1)}, f32[4,128,128]{1,2,0:T(8,128)S(1)}, u32[]{:S(2)}, u32[]{:S(2)}) %collective-permute-start.12) | collective-permute-done | bytes 262176 | tf_op jit(solution)/shard_map/ppermute | solution.py:14
  85.3 3.4 %collective-permute-start.13 = (f32[4,128,128]{1,2,0:T(8,128)S(1)}, f32[4,128,128]{1,2,0:T(8,128)S(1)}, u32[]{:S(2)}, u32[]{:S(2)}) collective-permute-start(f32[4,128,128]{1,2,0:T(8,128)S(1)} %collective-permute-done.12), channel_id=1, source_target_pairs={{4,0},{8,4},{12,8},{16,12},{20,16},{24,20},{28,24},{5,1},{9,5},{13... | collective-permute-start | bytes 786440 | tf_op jit(solution)/shard_map/ppermute | solution.py:14
  89.1 5.4 %collective-permute-done.13 = f32[4,128,128]{1,2,0:T(8,128)S(1)} collective-permute-done((f32[4,128,128]{1,2,0:T(8,128)S(1)}, f32[4,128,128]{1,2,0:T(8,128)S(1)}, u32[]{:S(2)}, u32[]{:S(2)}) %collective-permute-start.13) | collective-permute-done | bytes 262176 | tf_op jit(solution)/shard_map/ppermute | solution.py:14
  94.5 1.3 collective-permute-start.14
  96.6 0.8 copy.29
  97.4 3.6 %all-to-all-start = ((bf16[2,128,512]{1,2,0:T(8,128)(2,1)}), bf16[2,128,512]{1,2,0:T(8,128)(2,1)S(1)}, u32[]{:S(2)}, u32[]{:S(2)}) async-start(bf16[2,128,512]{1,2,0:T(8,128)(2,1)} %pad_maximum_fusion), calls=%async_computation | async-start | bytes 524288 | tf_op jit(solution)/shard_map/all_to_all | solution.py:86
  101.0 36.9 %psum.7 = f32[4,128]{1,0:T(4,128)S(1)} all-reduce(f32[4,128]{1,0:T(4,128)S(1)} %get-tuple-element.10), channel_id=1, replica_groups=mesh['seq'=8,'head'=2,'dp'=2] {'seq','dp'}, use_global_device_ids=true, to_apply=%region_3.4 | all-reduce | flops 512 | bytes 4096 | tf_op jit(solution)/shard_map/psum | solution.py:102
  138.1 1.0 fusion.10
  139.1 1.3 collective-permute-start.15
  141.0 1.3 convolution_bitcast_fusion
  142.3 13.4 %collective-permute-done.15 = f32[4,128,128]{1,2,0:T(8,128)S(1)} collective-permute-done((f32[4,128,128]{1,2,0:T(8,128)S(1)}, f32[4,128,128]{1,2,0:T(8,128)S(1)}, u32[]{:S(2)}, u32[]{:S(2)}) %collective-permute-start.15) | collective-permute-done | bytes 262176 | tf_op jit(solution)/shard_map/ppermute | solution.py:14
  156.2 0.8 copy.31
  157.4 0.8 copy.30
  158.3 3.7 %fusion = bf16[1,128,2048]{2,1,0:T(8,128)(2,1)} fusion(bf16[128,1024]{0,1:T(8,128)(2,1)S(1)} %bitcast.77, bf16[1024,2048]{1,0:T(8,128)(2,1)} %all-gather.2.cloned.1.call-done), kind=kOutput, calls=%fused_computation.1 | convolution fusion | flops 537133056 | bytes 4980736 | tf_op jit(solution)/shard_map/dot_general | solution.py:91
  (50 shorter events, 6.3 us)
Async XLA Ops:
  7.2 32.8 %copy-start = (bf16[1,256,2048]{2,1,0:T(8,128)(2,1)S(1)}, bf16[1,256,2048]{2,1,0:T(8,128)(2,1)}, u32[]{:S(2)}) copy-start(bf16[1,256,2048]{2,1,0:T(8,128)(2,1)} %param.13) | copy-start | bytes 3145732
  7.2 23.1 %copy-start.2 = (bf16[1,256,512]{2,1,0:T(8,128)(2,1)S(1)}, bf16[1,256,512]{2,1,0:T(8,128)(2,1)}, u32[]{:S(2)}) copy-start(bf16[1,256,512]{2,1,0:T(8,128)(2,1)} %param.7) | copy-start | bytes 786436
  7.2 151.1 %all-gather.2.cloned.1.call-start = ((), (), s32[]{:S(2)}) async-start(), calls=%async_computation.1 | async-start | bytes 6291456 | tf_op jit(solution)/shard_map/all_gather | solution.py:93
  10.5 9.1 %collective-permute-start.4 = (f32[4,128,128]{2,1,0:T(8,128)S(1)}, f32[4,128,128]{2,1,0:T(8,128)S(1)}, u32[]{:S(2)}, u32[]{:S(2)}) collective-permute-start(f32[4,128,128]{2,1,0:T(8,128)S(1)} %get-tuple-element.16), channel_id=1, source_target_pairs={{0,4},{4,8},{8,12},{12,16},{16,20},{20,24},{24,28},{1,5},{5,9},{9,... | collective-permute-start | bytes 786440 | tf_op jit(solution)/shard_map/ppermute | solution.py:14
  19.5 17.2 %collective-permute-start.5 = (f32[4,128,128]{2,1,0:T(8,128)S(1)}, f32[4,128,128]{2,1,0:T(8,128)S(1)}, u32[]{:S(2)}, u32[]{:S(2)}) collective-permute-start(f32[4,128,128]{2,1,0:T(8,128)S(1)} %collective-permute-done.4), channel_id=1, source_target_pairs={{0,4},{4,8},{8,12},{12,16},{16,20},{20,24},{24,28},{1,5},{5,9},{9,... | collective-permute-start | bytes 786440 | tf_op jit(solution)/shard_map/ppermute | solution.py:14
  23.6 6.8 %collective-permute-start = (f32[1]{0:T(128)}, f32[1]{0:T(128)}, u32[]{:S(2)}, u32[]{:S(2)}) collective-permute-start(f32[1]{0:T(128)} %bitcast.1), channel_id=1, source_target_pairs={{0,4},{4,8},{8,12},{12,16},{16,20},{20,24},{24,28},{1,5},{5,9},{9,... | collective-permute-start | bytes 20 | tf_op jit(solution)/shard_map/ppermute | solution.py:14
  27.6 25.3 %collective-permute-start.8 = (f32[1]{0:T(128)}, f32[1]{0:T(128)}, u32[]{:S(2)}, u32[]{:S(2)}) collective-permute-start(f32[1]{0:T(128)} %bitcast.1), channel_id=1, source_target_pairs={{4,0},{8,4},{12,8},{16,12},{20,16},{24,20},{28,24},{5,1},{9,5},{13... | collective-permute-start | bytes 20 | tf_op jit(solution)/shard_map/ppermute | solution.py:14
  30.4 5.0 %collective-permute-start.1 = (f32[1]{0:T(128)}, f32[1]{0:T(128)}, u32[]{:S(2)}, u32[]{:S(2)}) collective-permute-start(f32[1]{0:T(128)} %collective-permute-done), channel_id=1, source_target_pairs={{0,4},{4,8},{8,12},{12,16},{16,20},{20,24},{24,28},{1,5},{5,9},{9,... | collective-permute-start | bytes 20 | tf_op jit(solution)/shard_map/ppermute | solution.py:14
  36.8 39.8 %copy-start.3 = (f32[4,128]{1,0:T(4,128)S(1)}, f32[4,128]{1,0:T(4,128)}, u32[]{:S(2)}) copy-start(f32[4,128]{1,0:T(4,128)} %param.11) | copy-start | bytes 6148
  36.8 11.6 %collective-permute-start.6 = (f32[4,128,128]{2,1,0:T(8,128)S(1)}, f32[4,128,128]{2,1,0:T(8,128)S(1)}, u32[]{:S(2)}, u32[]{:S(2)}) collective-permute-start(f32[4,128,128]{2,1,0:T(8,128)S(1)} %fusion.14), channel_id=1, source_target_pairs={{0,8},{4,12},{8,16},{12,20},{16,24},{20,28},{1,9},{5,13},{9,17},{1... | collective-permute-start | bytes 786440 | tf_op jit(solution)/shard_map/ppermute | solution.py:14
  43.9 3.9 %collective-permute-start.2 = (f32[1]{0:T(128)}, f32[1]{0:T(128)}, u32[]{:S(2)}, u32[]{:S(2)}) collective-permute-start(f32[1]{0:T(128)} %select_n.117), channel_id=1, source_target_pairs={{0,8},{4,12},{8,16},{12,20},{16,24},{20,28},{1,9},{5,13},{9,17},{1... | collective-permute-start | bytes 20 | tf_op jit(solution)/shard_map/ppermute | solution.py:14
  48.4 27.6 %collective-permute-start.7 = (f32[4,128,128]{2,1,0:T(8,128)S(1)}, f32[4,128,128]{2,1,0:T(8,128)S(1)}, u32[]{:S(2)}, u32[]{:S(2)}) collective-permute-start(f32[4,128,128]{2,1,0:T(8,128)S(1)} %fusion.13), channel_id=1, source_target_pairs={{0,16},{4,20},{8,24},{12,28},{1,17},{5,21},{9,25},{13,29},{2,18},{... | collective-permute-start | bytes 786440 | tf_op jit(solution)/shard_map/ppermute | solution.py:14
  53.0 5.5 %collective-permute-start.9 = (f32[1]{0:T(128)}, f32[1]{0:T(128)}, u32[]{:S(2)}, u32[]{:S(2)}) collective-permute-start(f32[1]{0:T(128)} %collective-permute-done.8), channel_id=1, source_target_pairs={{4,0},{8,4},{12,8},{16,12},{20,16},{24,20},{28,24},{5,1},{9,5},{13... | collective-permute-start | bytes 20 | tf_op jit(solution)/shard_map/ppermute | solution.py:14
  59.8 8.3 %collective-permute-start.10 = (f32[1]{0:T(128)}, f32[1]{0:T(128)}, u32[]{:S(2)}, u32[]{:S(2)}) collective-permute-start(f32[1]{0:T(128)} %select_n.135), channel_id=1, source_target_pairs={{8,0},{12,4},{16,8},{20,12},{24,16},{28,20},{9,1},{13,5},{17,9},{2... | collective-permute-start | bytes 20 | tf_op jit(solution)/shard_map/ppermute | solution.py:14
  62.9 7.8 %collective-permute-start.3 = (f32[1]{0:T(128)}, f32[1]{0:T(128)}, u32[]{:S(2)}, u32[]{:S(2)}) collective-permute-start(f32[1]{0:T(128)} %select_n.118), channel_id=1, source_target_pairs={{0,16},{4,20},{8,24},{12,28},{1,17},{5,21},{9,25},{13,29},{2,18},{... | collective-permute-start | bytes 20 | tf_op jit(solution)/shard_map/ppermute | solution.py:14
  68.8 5.3 %collective-permute-start.11 = (f32[1]{0:T(128)}, f32[1]{0:T(128)}, u32[]{:S(2)}, u32[]{:S(2)}) collective-permute-start(f32[1]{0:T(128)} %select_n.136), channel_id=1, source_target_pairs={{16,0},{20,4},{24,8},{28,12},{17,1},{21,5},{25,9},{29,13},{18,2},{... | collective-permute-start | bytes 20 | tf_op jit(solution)/shard_map/ppermute | solution.py:14
  77.3 8.0 %collective-permute-start.12 = (f32[4,128,128]{1,2,0:T(8,128)S(1)}, f32[4,128,128]{1,2,0:T(8,128)S(1)}, u32[]{:S(2)}, u32[]{:S(2)}) collective-permute-start(f32[4,128,128]{1,2,0:T(8,128)S(1)} %multiply_bitcast_fusion), channel_id=1, source_target_pairs={{4,0},{8,4},{12,8},{16,12},{20,16},{24,20},{28,24},{5,1},{9,5},{13... | collective-permute-start | bytes 786440 | tf_op jit(solution)/shard_map/ppermute | solution.py:14
  81.6 7.6 %copy-start.1 = (bf16[4,256,256]{2,1,0:T(8,128)(2,1)}, bf16[4,256,256]{2,1,0:T(8,128)(2,1)S(1)}, u32[]{:S(2)}) copy-start(bf16[4,256,256]{2,1,0:T(8,128)(2,1)S(1)} %fusion.2) | copy-start | bytes 1572868
  85.3 9.2 %collective-permute-start.13 = (f32[4,128,128]{1,2,0:T(8,128)S(1)}, f32[4,128,128]{1,2,0:T(8,128)S(1)}, u32[]{:S(2)}, u32[]{:S(2)}) collective-permute-start(f32[4,128,128]{1,2,0:T(8,128)S(1)} %collective-permute-done.12), channel_id=1, source_target_pairs={{4,0},{8,4},{12,8},{16,12},{20,16},{24,20},{28,24},{5,1},{9,5},{13... | collective-permute-start | bytes 786440 | tf_op jit(solution)/shard_map/ppermute | solution.py:14
  94.5 43.5 %collective-permute-start.14 = (f32[4,128,128]{1,2,0:T(8,128)S(1)}, f32[4,128,128]{1,2,0:T(8,128)}, u32[]{:S(2)}, u32[]{:S(2)}) collective-permute-start(f32[4,128,128]{1,2,0:T(8,128)S(1)} %fusion.11), channel_id=1, source_target_pairs={{8,0},{12,4},{16,8},{20,12},{24,16},{28,20},{9,1},{13,5},{17,9},{2... | collective-permute-start | bytes 786440 | tf_op jit(solution)/shard_map/ppermute | solution.py:14
  97.4 60.9 %all-to-all-start = ((bf16[2,128,512]{1,2,0:T(8,128)(2,1)}), bf16[2,128,512]{1,2,0:T(8,128)(2,1)S(1)}, u32[]{:S(2)}, u32[]{:S(2)}) async-start(bf16[2,128,512]{1,2,0:T(8,128)(2,1)} %pad_maximum_fusion), calls=%async_computation | async-start | bytes 524288 | tf_op jit(solution)/shard_map/all_to_all | solution.py:86
  139.1 16.6 %collective-permute-start.15 = (f32[4,128,128]{1,2,0:T(8,128)S(1)}, f32[4,128,128]{1,2,0:T(8,128)S(1)}, u32[]{:S(2)}, u32[]{:S(2)}) collective-permute-start(f32[4,128,128]{1,2,0:T(8,128)S(1)} %fusion.10), channel_id=1, source_target_pairs={{16,0},{20,4},{24,8},{28,12},{17,1},{21,5},{25,9},{29,13},{18,2},{... | collective-permute-start | bytes 786440 | tf_op jit(solution)/shard_map/ppermute | solution.py:14
Sparse Core Ops, SparseCore 0:
  30.4 59.8 all-gather.1
